TPU v7x, 32 devices: a whole 2x2x4 slice. The times are simulated.
32 devices in a mesh: dp: 8 (over z, x), ctx: 4 (over y, core).
Axes of the slice: x: 2, y: 2, z: 4, core: 2. Of those that a mesh axis runs over, the one named last changes fastest.
Arguments:
- tokens: bfloat16 [4096, 1024], P(('dp', 'ctx')), may hold values from -6 to 6
- cotangent: bfloat16 [4096, 1024], P(('dp', 'ctx')), may hold values from -6 to 6
- segment_ids: int32 [8, 512], P('dp'), may hold values from 0 to 3, never falling along the last dimension, each value on 1 to 256 neighbouring positions
- tract_order: int32 [8, 8], P('dp'), may hold values from 0 to 7, each once within a row
- qkv_weight: bfloat16 [1024, 3072], P(('dp', 'ctx')), may hold values from -0.1875 to 0.1875
- out_weight: bfloat16 [1024, 1024], P(('dp', 'ctx')), may hold values from -2 to 2
- up_weight: bfloat16 [1024, 4096], P(('dp', 'ctx')), may hold values from -0.1875 to 0.1875
- down_weight: bfloat16 [4096, 1024], P(('dp', 'ctx')), may hold values from -0.09375 to 0.09375
- norm_gain: bfloat16 [2, 1024], P(None, ('dp', 'ctx')), may hold values from 0.5 to 1.5
- norm_shift: bfloat16 [2, 1024], P(None, ('dp', 'ctx')), may hold values from -4 to 4
- proj_bias: bfloat16 [4, 1024], P(None, ('dp', 'ctx')), may hold values from -6 to 6
- up_bias: bfloat16 [4096], P(('dp', 'ctx')), may hold values from -6 to 6
Outputs:
- block_out: float32 [4096, 1024], P(('dp', 'ctx'))
- input_grad: float32 [4096, 1024], P(('dp', 'ctx'))
- qkv_weight_grad: float32 [1024, 3072], P(('dp', 'ctx'))
- out_weight_grad: float32 [1024, 1024], P(('dp', 'ctx'))
- up_weight_grad: float32 [1024, 4096], P(('dp', 'ctx'))
- down_weight_grad: float32 [4096, 1024], P(('dp', 'ctx'))
- norm_gain_grad: float32 [2, 1024], P(None, ('dp', 'ctx'))
- norm_shift_grad: float32 [2, 1024], P(None, ('dp', 'ctx'))
- proj_bias_grad: float32 [4, 1024], P(None, ('dp', 'ctx'))
- up_bias_grad: float32 [4096], P(('dp', 'ctx'))
Inputs may be any that keep to these rules, and one draw needn't show every extreme that they name: `segment_ids`: along each row the ids never fall; one document covers at most 256 positions of a row. `tract_order`: each row is a permutation: every place 0 to 7 is named once.
All inputs are finite; a program needn't handle non-finite values.
Results may differ from a plain program's by a relative error of at most 0.011.
Values may be sent and summed in bfloat16 or wider, within the bound.
A program may use at most 256 MiB of HBM per device.

v0:
```python
import jax
import jax.numpy as jnp
from jax import lax
from jax.sharding import PartitionSpec as P

HEAD_DIM = 64
EPSILON = 1e-05
GELU_COEF = 0.7978845608028654


def gelu_parts(inputs):
    cubed_part = inputs * inputs * inputs
    tanh_part = jnp.tanh(GELU_COEF * (inputs + 0.044715 * cubed_part))
    values = 0.5 * inputs * (1.0 + tanh_part)
    slopes = 0.5 * (1.0 + tanh_part) + 0.5 * inputs * (1.0 - tanh_part * tanh_part) * GELU_COEF * (
        1.0 + 3.0 * 0.044715 * inputs * inputs
    )
    return (values, slopes)


def norm_parts(values):
    centred = values - jnp.mean(values, axis=-1, keepdims=True)
    inverse = lax.rsqrt(jnp.mean(centred * centred, axis=-1, keepdims=True) + EPSILON)
    return (centred * inverse, inverse)


def norm_back(grads, normed, inverse, gain_row):
    scaled = grads * gain_row
    return inverse * (
        scaled
        - jnp.mean(scaled, axis=-1, keepdims=True)
        - normed * jnp.mean(scaled * normed, axis=-1, keepdims=True)
    )


def outer_sum(former, latter):
    return lax.dot_general(
        former, latter, (((0,), (0,)), ((), ())), preferred_element_type=jnp.float32
    )


def back_product(former, latter):
    return lax.dot_general(
        former, latter, (((1,), (1,)), ((), ())), preferred_element_type=jnp.float32
    )


def shards(
    tokens,
    cotangent,
    segment_ids,
    tract_order,
    qkv_weight,
    out_weight,
    up_weight,
    down_weight,
    norm_gain,
    norm_shift,
    proj_bias,
    up_bias,
):
    both = ("dp", "ctx")
    dp_count = lax.axis_size("dp")
    ctx_count = lax.axis_size("ctx")
    here = lax.axis_index("ctx")
    row_count, width = tokens.shape
    span = row_count * ctx_count
    block_rows = segment_ids.shape[1] // tract_order.shape[1]
    own_rows = qkv_weight.shape[0]
    own_hidden = up_bias.shape[0]
    own_feats = norm_gain.shape[1]
    hidden = dp_count * own_hidden
    part = width // ctx_count
    heads = part // HEAD_DIM
    attn_scale = HEAD_DIM ** (-0.5)
    smalls = jnp.concatenate(
        [norm_gain.reshape(-1), norm_shift.reshape(-1), proj_bias.reshape(-1), up_bias]
    )[None]
    smalls = lax.all_gather(smalls, both, axis=0, tiled=True).astype(jnp.float32)

    def spread(first, count):
        piece = smalls[:, first * own_feats : (first + count) * own_feats]
        return piece.reshape(-1, count, own_feats).transpose(1, 0, 2).reshape(count, width)

    gains = spread(0, 2)
    shifts = spread(2, 2)
    biases = spread(4, 4)
    up_shift = lax.dynamic_index_in_dim(
        smalls[:, 8 * own_feats :].reshape(dp_count, ctx_count, own_hidden), here, 1, False
    ).reshape(hidden)
    qkv_cols = (
        qkv_weight.reshape(own_rows, 3, ctx_count, part)
        .transpose(2, 0, 1, 3)
        .reshape(ctx_count, own_rows, 3 * part)
    )
    up_cols = (
        up_weight.reshape(own_rows, dp_count, ctx_count, own_hidden)
        .transpose(2, 0, 1, 3)
        .reshape(ctx_count, own_rows, hidden)
    )
    swapped = lax.all_to_all(
        jnp.concatenate([qkv_cols, up_cols], axis=2), "ctx", 0, 0, tiled=True
    ).reshape(ctx_count * own_rows, 3 * part + hidden)
    streams = lax.all_gather(jnp.stack([tokens, cotangent]), "ctx", axis=1, tiled=True)
    qkv_part = lax.all_gather(swapped[:, : 3 * part], "dp", axis=0, tiled=True)
    out_full = lax.all_gather(out_weight, both, axis=0, tiled=True)
    up_part = lax.all_gather(swapped[:, 3 * part :], "dp", axis=0, tiled=True)
    down_part = lax.all_gather(down_weight, "dp", axis=0, tiled=True)
    tokens_span, cot_span = (streams[0], streams[1])
    block_ranks = tract_order[0]
    positions = (
        block_ranks[:, None] * block_rows + jnp.arange(block_rows, dtype=jnp.int32)[None, :]
    ).reshape(-1)
    segments = jnp.take(segment_ids[0].reshape(-1, block_rows), block_ranks, axis=0).reshape(-1)
    allowed = (positions[None, :] <= positions[:, None]) & (segments[None, :] == segments[:, None])
    normed_span, _ = norm_parts(tokens_span.astype(jnp.float32))
    normed_in = (normed_span * gains[0] + shifts[0]).astype(jnp.bfloat16)
    projected = jnp.dot(normed_in, qkv_part, preferred_element_type=jnp.float32)
    query_shift = lax.dynamic_slice_in_dim(biases[0], here * part, part)
    value_shift = lax.dynamic_slice_in_dim(biases[1], here * part, part)
    query_heads = (
        (projected[:, :part] + query_shift).astype(jnp.bfloat16).reshape(span, heads, HEAD_DIM)
    )
    key_heads = projected[:, part : 2 * part].astype(jnp.bfloat16).reshape(span, heads, HEAD_DIM)
    value_heads = (
        (projected[:, 2 * part :] + value_shift).astype(jnp.bfloat16).reshape(span, heads, HEAD_DIM)
    )
    scores = (
        jnp.einsum("qhd,khd->hqk", query_heads, key_heads, preferred_element_type=jnp.float32)
        * attn_scale
    )
    exp_weights = jnp.where(allowed[None], jnp.exp(scores), 0.0)
    denominator = jnp.sum(exp_weights, axis=-1)
    numerator = jnp.einsum(
        "hqk,khd->qhd",
        exp_weights.astype(jnp.bfloat16),
        value_heads,
        preferred_element_type=jnp.float32,
    )
    att_heads = (numerator / denominator.T[:, :, None]).astype(jnp.bfloat16)
    log_total = jnp.log(denominator)
    att_part = att_heads.reshape(span, part)
    attended = lax.all_to_all(att_part, "ctx", 0, 1, tiled=True)
    resid_in = tokens.astype(jnp.float32)
    resid_mid = (
        resid_in + jnp.dot(attended, out_full, preferred_element_type=jnp.float32) + biases[2]
    )
    normed_two, inverse_two = norm_parts(resid_mid)
    normed_mid = lax.all_gather(
        (normed_two * gains[1] + shifts[1]).astype(jnp.bfloat16), "ctx", axis=0, tiled=True
    )
    pre_act = jnp.dot(normed_mid, up_part, preferred_element_type=jnp.float32) + up_shift
    activated, slopes = gelu_parts(pre_act)
    act_rows = activated.astype(jnp.bfloat16)
    grad_top = cotangent.astype(jnp.float32)
    grad_act = back_product(cot_span, down_part)
    grad_pre = grad_act * slopes
    grad_pre_low = grad_pre.astype(jnp.bfloat16)
    grad_norm_two = lax.psum_scatter(
        back_product(grad_pre_low, up_part).astype(jnp.bfloat16),
        "ctx",
        scatter_dimension=0,
        tiled=True,
    ).astype(jnp.float32)
    block_out = (
        resid_mid
        + lax.psum_scatter(
            jnp.dot(act_rows, down_part, preferred_element_type=jnp.float32).astype(jnp.bfloat16),
            "ctx",
            scatter_dimension=0,
            tiled=True,
        ).astype(jnp.float32)
        + biases[3]
    )
    grad_mid = grad_top + norm_back(grad_norm_two, normed_two, inverse_two, gains[1])
    mid_span = lax.all_gather(grad_mid.astype(jnp.bfloat16), "ctx", axis=0, tiled=True)
    out_rows = lax.dynamic_slice_in_dim(out_full, here * part, part)
    grad_att = back_product(mid_span, out_rows).astype(jnp.bfloat16).reshape(span, heads, HEAD_DIM)
    delta_rows = jnp.sum(grad_att.astype(jnp.float32) * att_heads.astype(jnp.float32), axis=-1).T
    soft_weights = jnp.where(allowed[None], jnp.exp(scores - log_total[:, :, None]), 0.0)
    grad_value = jnp.einsum(
        "hqk,qhd->khd",
        soft_weights.astype(jnp.bfloat16),
        grad_att,
        preferred_element_type=jnp.float32,
    ).reshape(span, part)
    grad_probs = jnp.einsum(
        "qhd,khd->hqk", grad_att, value_heads, preferred_element_type=jnp.float32
    )
    grad_scores = (soft_weights * (grad_probs - delta_rows[:, :, None])).astype(jnp.bfloat16)
    grad_query = (
        jnp.einsum(
            "hqk,khd->qhd", grad_scores, key_heads, preferred_element_type=jnp.float32
        ).reshape(span, part)
        * attn_scale
    )
    grad_key = (
        jnp.einsum(
            "hqk,qhd->khd", grad_scores, query_heads, preferred_element_type=jnp.float32
        ).reshape(span, part)
        * attn_scale
    )
    grad_proj = jnp.concatenate([grad_query, grad_key, grad_value], axis=1).astype(jnp.bfloat16)
    grad_norm_one = lax.psum_scatter(
        back_product(grad_proj, qkv_part).astype(jnp.bfloat16),
        "ctx",
        scatter_dimension=0,
        tiled=True,
    ).astype(jnp.float32)
    normed_one, inverse_one = norm_parts(resid_in)
    input_grad = grad_mid + norm_back(grad_norm_one, normed_one, inverse_one, gains[0])

    def over_dp(former, latter):
        return lax.psum_scatter(
            outer_sum(former, latter).astype(jnp.bfloat16), "dp", scatter_dimension=0, tiled=True
        )

    down_grad = over_dp(act_rows, cot_span).astype(jnp.float32)
    up_rows = over_dp(normed_mid, grad_pre_low)
    outw_rows = over_dp(att_part, mid_span)
    qkv_rows = over_dp(normed_in, grad_proj)
    outw_grad = lax.ppermute(
        outw_rows,
        both,
        [(d * ctx_count + c, c * dp_count + d) for d in range(dp_count) for c in range(ctx_count)],
    ).astype(jnp.float32)
    returned = lax.all_to_all(
        jnp.concatenate([qkv_rows, up_rows], axis=1).reshape(ctx_count, own_rows, -1),
        "ctx",
        0,
        0,
        tiled=True,
    ).astype(jnp.float32)
    qkv_grad = (
        returned[:, :, : 3 * part]
        .reshape(ctx_count, own_rows, 3, part)
        .transpose(1, 2, 0, 3)
        .reshape(own_rows, 3 * width)
    )
    up_grad = (
        returned[:, :, 3 * part :]
        .reshape(ctx_count, own_rows, dp_count, own_hidden)
        .transpose(1, 2, 0, 3)
        .reshape(own_rows, hidden * ctx_count)
    )

    def placed(sums):
        return lax.dynamic_update_slice_in_dim(
            jnp.zeros((width,), jnp.float32), sums, here * part, 0
        )

    feature_sums = jnp.stack(
        [
            jnp.sum(grad_norm_one * normed_one, axis=0),
            jnp.sum(grad_norm_two * normed_two, axis=0),
            jnp.sum(grad_norm_one, axis=0),
            jnp.sum(grad_norm_two, axis=0),
            placed(jnp.sum(grad_query, axis=0)),
            placed(jnp.sum(grad_value, axis=0)),
            jnp.sum(grad_mid, axis=0),
            jnp.sum(grad_top, axis=0),
        ]
    )
    hidden_sums = lax.dynamic_update_slice_in_dim(
        jnp.zeros((dp_count, ctx_count, own_hidden), jnp.float32),
        jnp.sum(grad_pre, axis=0).reshape(dp_count, 1, own_hidden),
        here,
        1,
    ).reshape(dp_count * ctx_count, own_hidden)
    packed = jnp.concatenate(
        [
            feature_sums.reshape(8, -1, own_feats).transpose(1, 0, 2).reshape(-1, 8 * own_feats),
            hidden_sums,
        ],
        axis=1,
    )
    owned = lax.psum_scatter(packed, both, scatter_dimension=0, tiled=True)[0]
    rows = owned[: 8 * own_feats].reshape(8, own_feats)
    return (
        block_out,
        input_grad,
        qkv_grad,
        outw_grad,
        up_grad,
        down_grad,
        rows[0:2],
        rows[2:4],
        rows[4:8],
        owned[8 * own_feats :],
    )


def solution(mesh):
    return jax.shard_map(
        shards,
        mesh=mesh,
        in_specs=(
            P(("dp", "ctx"), None),
            P(("dp", "ctx"), None),
            P("dp", None),
            P("dp", None),
            P(("dp", "ctx"), None),
            P(("dp", "ctx"), None),
            P(("dp", "ctx"), None),
            P(("dp", "ctx"), None),
            P(None, ("dp", "ctx")),
            P(None, ("dp", "ctx")),
            P(None, ("dp", "ctx")),
            P(("dp", "ctx")),
        ),
        out_specs=(
            P(("dp", "ctx"), None),
            P(("dp", "ctx"), None),
            P(("dp", "ctx"), None),
            P(("dp", "ctx"), None),
            P(("dp", "ctx"), None),
            P(("dp", "ctx"), None),
            P(None, ("dp", "ctx")),
            P(None, ("dp", "ctx")),
            P(None, ("dp", "ctx")),
            P(("dp", "ctx")),
        ),
        check_vma=False,
    )
```

profile of v0, /device:TPU:0, one launch (start us, length us, event | category | flops | bytes accessed | tf_op | source)
XLA Modules:
  0.0 666.1 jit_solution(16236123342175305526)
XLA Ops:
  11.1 13.2 %all_to_all.29 = bf16[4,32,1792]{2,1,0:T(8,128)(2,1)S(1)} all-to-all(bf16[4,32,1792]{2,1,0:T(8,128)(2,1)S(1)} %pad_maximum_fusion.2), channel_id=1, replica_groups=mesh['dp'=8,'ctx'=4] {'ctx'}, dimensions={0} | all-to-all | bytes 917504 | tf_op jit(solution)/shard_map/all_to_all | solution.py:101
  26.2 40.8 %all-gather.1 = bf16[32,1,384]{2,1,0:T(2,128)(2,1)S(1)} all-gather(bf16[1,1,384]{2,1,0:T(2,128)(2,1)S(1)} %reshape.405), channel_id=2, replica_groups=mesh['dp'=8,'ctx'=4] {'dp','ctx'}, dimensions={0}, use_global_device_ids=true | all-gather | bytes 25344 | tf_op jit(solution)/shard_map/all_gather | solution.py:79
  74.7 8.8 %all-gather.12.cloned.1.call-done = bf16[1024,768]{1,0:T(8,128)(2,1)} async-done(((bf16[128,768]{1,0:T(8,128)(2,1)}), bf16[1024,768]{1,0:T(8,128)(2,1)}) %all-gather.12.cloned.1.call-update) | async-done | bytes 1572880 | tf_op jit(solution)/shard_map/all_gather | solution.py:105
  83.5 2.5 fusion.73
  91.6 3.4 all-to-all-start.1
  95.3 5.7 all-to-all-done.1
  101.0 40.1 %all-gather.14.cloned.1.call-done = bf16[1024,1024]{1,0:T(8,128)(2,1)} async-done(((bf16[32,1024]{1,0:T(8,128)(2,1)}), bf16[1024,1024]{1,0:T(8,128)(2,1)}) %all-gather.14.cloned.1.call-update) | async-done | bytes 2097168 | tf_op jit(solution)/shard_map/all_gather | solution.py:106
  141.1 2.1 fusion.80
  145.2 46.4 %all-gather.18.cloned.1.call-done = bf16[1024,1024]{1,0:T(8,128)(2,1)} async-done(((bf16[128,1024]{1,0:T(8,128)(2,1)}), bf16[1024,1024]{1,0:T(8,128)(2,1)}) %all-gather.18.cloned.1.call-update) | async-done | bytes 2097168 | tf_op jit(solution)/shard_map/all_gather | solution.py:107
  191.6 17.2 %all-gather.16.cloned.1.call-done = bf16[512,1024]{1,0:T(8,128)(2,1)} async-done(((bf16[128,1024]{1,0:T(8,128)(2,1)}), bf16[512,1024]{1,0:T(8,128)(2,1)}) %all-gather.16.cloned.1.call-update) | async-done | bytes 1048592 | tf_op jit(solution)/shard_map/all_gather | solution.py:149
  208.9 4.6 fusion.82
  213.4 46.5 %all-gather.20.cloned.1.call-done = bf16[1024,1024]{1,0:T(8,128)(2,1)} async-done(((bf16[128,1024]{1,0:T(8,128)(2,1)}), bf16[1024,1024]{1,0:T(8,128)(2,1)}) %all-gather.20.cloned.1.call-update) | async-done | bytes 2097168 | tf_op jit(solution)/shard_map/all_gather | solution.py:108
  260.0 4.8 fusion.81
  265.8 2.3 convolution_convert_fusion.4
  268.1 4.7 convolution_convert_fusion.5
  273.0 18.6 %reduce-scatter.10.cloned.1.call-done = bf16[128,1024]{1,0:T(8,128)(2,1)} async-done(((bf16[512,1024]{1,0:T(8,128)(2,1)}), bf16[128,1024]{1,0:T(8,128)(2,1)}) %reduce-scatter.10.cloned.1.call-update) | async-done | bytes 262160 | tf_op jit(solution)/shard_map/reduce_scatter | solution.py:159
  292.8 26.1 %reduce-scatter.8.cloned.1.call-done = bf16[128,1024]{1,0:T(8,128)(2,1)} async-done(((bf16[512,1024]{1,0:T(8,128)(2,1)}), bf16[128,1024]{1,0:T(8,128)(2,1)}) %reduce-scatter.8.cloned.1.call-update) | async-done | bytes 262160 | tf_op jit(solution)/shard_map/reduce_scatter | solution.py:167
  318.9 2.2 fusion.75
  321.9 16.8 %all-gather.22.cloned.1.call-done = bf16[512,1024]{1,0:T(8,128)(2,1)} async-done(((bf16[128,1024]{1,0:T(8,128)(2,1)}), bf16[512,1024]{1,0:T(8,128)(2,1)}) %all-gather.22.cloned.1.call-update) | async-done | bytes 1048592 | tf_op jit(solution)/shard_map/all_gather | solution.py:176
  338.7 2.5 convolution_convert_fusion.6
  341.3 4.6 convolution_convert_fusion
  348.7 3.8 multiply_convert_fusion
  358.8 4.2 convolution_convert_fusion.1
  363.0 3.4 convolution_convert_fusion.2
  368.6 36.6 %reduce-scatter.18.cloned.1.call-done = bf16[32,1024]{1,0:T(8,128)(2,1)} async-done(((bf16[256,1024]{1,0:T(8,128)(2,1)}), bf16[32,1024]{1,0:T(8,128)(2,1)}) %reduce-scatter.18.cloned.1.call-update) | async-done | bytes 65552 | tf_op jit(solution)/shard_map/reduce_scatter | solution.py:214
  407.5 68.8 %reduce-scatter.20.cloned.1.call-done = bf16[128,1024]{1,0:T(8,128)(2,1)} async-done(((bf16[1024,1024]{1,0:T(8,128)(2,1)}), bf16[128,1024]{1,0:T(8,128)(2,1)}) %reduce-scatter.20.cloned.1.call-update) | async-done | bytes 262160 | tf_op jit(solution)/shard_map/reduce_scatter | solution.py:214
  478.7 23.7 %reduce-scatter.12.cloned.1.call-done = bf16[128,1024]{1,0:T(8,128)(2,1)} async-done(((bf16[512,1024]{1,0:T(8,128)(2,1)}), bf16[128,1024]{1,0:T(8,128)(2,1)}) %reduce-scatter.12.cloned.1.call-update) | async-done | bytes 262160 | tf_op jit(solution)/shard_map/reduce_scatter | solution.py:204
  504.3 40.7 %all-reduce = f32[32,384]{1,0:T(8,128)S(1)} all-reduce(f32[32,384]{1,0:T(8,128)S(1)} %pad_maximum_fusion.6), channel_id=10, replica_groups=mesh['dp'=8,'ctx'=4] {'dp','ctx'}, use_global_device_ids=true, to_apply=%region_28.29.clone | all-reduce | flops 12288 | bytes 98304
  545.0 30.5 %reduce-scatter.16.cloned.1.call-done = bf16[128,1024]{1,0:T(8,128)(2,1)} async-done(((bf16[1024,1024]{1,0:T(8,128)(2,1)}), bf16[128,1024]{1,0:T(8,128)(2,1)}) %reduce-scatter.16.cloned.1.call-update) | async-done | bytes 262160 | tf_op jit(solution)/shard_map/reduce_scatter | solution.py:214
  575.4 67.8 %reduce-scatter.14.cloned.1.call-done = bf16[128,768]{1,0:T(8,128)(2,1)} async-done(((bf16[1024,768]{1,0:T(8,128)(2,1)}), bf16[128,768]{1,0:T(8,128)(2,1)}) %reduce-scatter.14.cloned.1.call-update) | async-done | bytes 196624 | tf_op jit(solution)/shard_map/reduce_scatter | solution.py:214
  645.0 3.5 all-to-all-start.2
  652.2 4.4 all-to-all-done.2
  (205 shorter events, 50.3 us)
Async XLA Ops:
  7.2 3.4 copy-start.14
  7.2 64.2 %all-gather.10.cloned.1.call-start = ((), (), s32[]{:S(2)}) async-start(), calls=%async_computation.10 | async-start | bytes 2621440 | tf_op jit(solution)/shard_map/all_gather | solution.py:104
  9.2 74.3 %all-gather.12.cloned.1.call-start = ((), (), s32[]{:S(2)}) async-start(), calls=%async_computation.11 | async-start | bytes 1769472 | tf_op jit(solution)/shard_map/all_gather | solution.py:105
  10.4 15.4 %copy-start.20 = (bf16[2,32]{1,0:T(2,128)(2,1)S(1)}, bf16[2,32]{1,0:T(2,128)(2,1)}, u32[]{:S(2)}) copy-start(bf16[2,32]{1,0:T(2,128)(2,1)} %param.20) | copy-start | bytes 388
  10.4 15.5 %copy-start.21 = (bf16[2,32]{1,0:T(2,128)(2,1)S(1)}, bf16[2,32]{1,0:T(2,128)(2,1)}, u32[]{:S(2)}) copy-start(bf16[2,32]{1,0:T(2,128)(2,1)} %param.21) | copy-start | bytes 388
  10.4 15.6 %copy-start.19 = (bf16[4,32]{1,0:T(4,128)(2,1)S(1)}, bf16[4,32]{1,0:T(4,128)(2,1)}, u32[]{:S(2)}) copy-start(bf16[4,32]{1,0:T(4,128)(2,1)} %param.22) | copy-start | bytes 772
  10.4 15.7 %copy-start.16 = (bf16[128]{0:T(256)(128)(2,1)S(1)}, bf16[128]{0:T(256)(128)(2,1)}, u32[]{:S(2)}) copy-start(bf16[128]{0:T(256)(128)(2,1)} %param.23) | copy-start | bytes 772
  10.7 58.0 %copy-start.15 = (s32[1,512]{1,0:T(1,128)S(1)}, s32[1,512]{1,0:T(1,128)}, u32[]{:S(2)}) copy-start(s32[1,512]{1,0:T(1,128)} %param.14) | copy-start | bytes 6148
  10.7 58.7 %copy-start.22 = (s32[1,8]{1,0:T(1,128)S(1)}, s32[1,8]{1,0:T(1,128)}, u32[]{:S(2)}) copy-start(s32[1,8]{1,0:T(1,128)} %param.15) | copy-start | bytes 100
  25.0 116.1 %all-gather.14.cloned.1.call-start = ((), (), s32[]{:S(2)}) async-start(), calls=%async_computation.12 | async-start | bytes 2162688 | tf_op jit(solution)/shard_map/all_gather | solution.py:106
  25.8 165.8 %all-gather.18.cloned.1.call-start = ((), (), s32[]{:S(2)}) async-start(), calls=%async_computation.14 | async-start | bytes 2359296 | tf_op jit(solution)/shard_map/all_gather | solution.py:107
  71.4 16.6 %copy-start.9 = (pred[512,512]{0,1:T(8,128)(4,1)}, pred[512,512]{0,1:T(8,128)(4,1)S(1)}, u32[]{:S(2)}) copy-start(pred[512,512]{0,1:T(8,128)(4,1)S(1)} %compare_and_fusion) | copy-start | bytes 786436
  71.4 12.0 %copy-start.1 = (bf16[2,512,1024]{2,1,0:T(8,128)(2,1)S(1)}, bf16[2,512,1024]{2,1,0:T(8,128)(2,1)}, u32[]{:S(2)}) copy-start(bf16[2,512,1024]{2,1,0:T(8,128)(2,1)} %all-gather.10.cloned.1.call-done) | copy-start | bytes 6291460
  89.9 51.2 %copy-start = (bf16[128,1024]{1,0:T(8,128)(2,1)S(1)}, bf16[128,1024]{1,0:T(8,128)(2,1)}, u32[]{:S(2)}) copy-start(bf16[128,1024]{1,0:T(8,128)(2,1)} %param.12) | copy-start | bytes 786436
  90.8 52.4 %copy-start.6 = (bf16[512,4,64]{0,2,1:T(8,128)(2,1)}, bf16[512,4,64]{0,2,1:T(8,128)(2,1)S(1)}, u32[]{:S(2)}) copy-start(bf16[512,4,64]{0,2,1:T(8,128)(2,1)S(1)} %fusion.37) | copy-start | bytes 786436
  91.6 9.4 %all-to-all-start.1 = ((bf16[4,128,256]{1,2,0:T(8,128)(2,1)}), bf16[4,128,256]{1,2,0:T(8,128)(2,1)S(1)}, u32[]{:S(2)}, u32[]{:S(2)}) async-start(bf16[4,128,256]{1,2,0:T(8,128)(2,1)} %copy.66), calls=%async_computation.1 | async-start | bytes 524288 | tf_op jit(solution)/shard_map/all_to_all | solution.py:143
  95.0 113.8 %all-gather.16.cloned.1.call-start = ((), (), s32[]{:S(2)}) async-start(), calls=%async_computation.13 | async-start | bytes 1310720 | tf_op jit(solution)/shard_map/all_gather | solution.py:149
  144.4 115.6 %all-gather.20.cloned.1.call-start = ((), (), s32[]{:S(2)}) async-start(), calls=%async_computation.15 | async-start | bytes 2359296 | tf_op jit(solution)/shard_map/all_gather | solution.py:108
  144.9 146.6 %reduce-scatter.10.cloned.1.call-start = ((), (), s32[]{:S(2)}) async-start(), calls=%async_computation.17 | async-start | bytes 1310720 | tf_op jit(solution)/shard_map/reduce_scatter | solution.py:159
  260.0 5.8 copy-start.17
  268.1 50.8 %reduce-scatter.8.cloned.1.call-start = ((), (), s32[]{:S(2)}) async-start(), calls=%async_computation.16 | async-start | bytes 1310720 | tf_op jit(solution)/shard_map/reduce_scatter | solution.py:167
  272.9 65.8 %all-gather.22.cloned.1.call-start = ((), (), s32[]{:S(2)}) async-start(), calls=%async_computation.18 | async-start | bytes 1310720 | tf_op jit(solution)/shard_map/all_gather | solution.py:176
  321.8 83.4 %reduce-scatter.18.cloned.1.call-start = ((), (), s32[]{:S(2)}) async-start(), calls=%async_computation.22 | async-start | bytes 589824 | tf_op jit(solution)/shard_map/reduce_scatter | solution.py:214
  341.2 135.0 %reduce-scatter.20.cloned.1.call-start = ((), (), s32[]{:S(2)}) async-start(), calls=%async_computation.23 | async-start | bytes 2359296 | tf_op jit(solution)/shard_map/reduce_scatter | solution.py:214
  345.9 2.8 copy-start.10
  345.9 156.6 %reduce-scatter.12.cloned.1.call-start = ((), (), s32[]{:S(2)}) async-start(), calls=%async_computation.19 | async-start | bytes 1310720 | tf_op jit(solution)/shard_map/reduce_scatter | solution.py:204
  348.7 3.8 copy-start.5
  358.7 216.7 %reduce-scatter.16.cloned.1.call-start = ((), (), s32[]{:S(2)}) async-start(), calls=%async_computation.21 | async-start | bytes 2359296 | tf_op jit(solution)/shard_map/reduce_scatter | solution.py:214
  363.0 280.2 %reduce-scatter.14.cloned.1.call-start = ((), (), s32[]{:S(2)}) async-start(), calls=%async_computation.20 | async-start | bytes 1769472 | tf_op jit(solution)/shard_map/reduce_scatter | solution.py:214
  405.2 72.8 %collective-permute-start = (bf16[32,1024]{1,0:T(8,128)(2,1)}, bf16[32,1024]{1,0:T(8,128)(2,1)S(1)}, u32[]{:S(2)}, u32[]{:S(2)}) collective-permute-start(bf16[32,1024]{1,0:T(8,128)(2,1)} %reduce-scatter.18.cloned.1.call-done), channel_id=1, source_target_pairs={{0,0},{1,8},{2,16},{3,24},{4,1},{5,9},{6,17},{7,25},{8,2},{9,10},{... | collective-permute-start | bytes 196616 | tf_op jit(solution)/shard_map/ppermute | solution.py:222
  502.5 148.7 %copy-start.8 = (bf16[128,1024]{1,0:T(8,128)(2,1)S(1)}, bf16[128,1024]{1,0:T(8,128)(2,1)}, u32[]{:S(2)}) copy-start(bf16[128,1024]{1,0:T(8,128)(2,1)} %reduce-scatter.12.cloned.1.call-done) | copy-start | bytes 786436
  645.0 11.6 %all-to-all-start.2 = ((bf16[4,32,1792]{2,1,0:T(8,128)(2,1)}), bf16[4,32,1792]{2,1,0:T(8,128)(2,1)S(1)}, u32[]{:S(2)}, u32[]{:S(2)}) async-start(bf16[4,32,1792]{2,1,0:T(8,128)(2,1)} %bitcast.30), calls=%async_computation.7 | async-start | bytes 917504 | tf_op jit(solution)/shard_map/all_to_all | solution.py:227
  (12 other events, 18.4 us)
Sparse Core Ops, SparseCore 0:
  10.1 25.9 all-gather.9
  38.8 44.5 all-gather.11
  86.3 54.7 all-gather.13
  143.6 47.9 all-gather.17
  193.6 15.2 all-gather.15
  210.8 49.0 all-gather.19
  268.2 23.2 reduce-scatter.9
  294.1 24.7 reduce-scatter.7
  321.9 16.6 all-gather.21
  342.4 62.7 reduce-scatter.17
  408.8 67.4 reduce-scatter.19
  478.6 23.7 reduce-scatter.11
  506.0 69.3 reduce-scatter.15
  578.7 64.4 reduce-scatter.13
where the time goes:
time: 667 us; the launch traced here: 666 us
  waiting for transfers between devices  459 us (69%)
  blocking collectives  94.7 us (14%)
  matrix products  47.9 us (7%)
  local copies, waits for them, and re-layouts  20.1 us (3%)
  other arithmetic  20 us (3%)
  between operations  14.6 us (2%)
  starting transfers between devices  9.33 us (1%)
    reduce_scatter x4, waiting for transfers between devices, over_dp(): lax.psum_scatter(outer_sum(former, latter).astype(jnp.bfloat16), 'dp', sc...  204 us
    all_gather x1, waiting for transfers between devices, shards(): down_part = lax.all_gather(down_weight, 'dp', axis=0, tiled=True)  46.5 us
    all_gather x1, waiting for transfers between devices, shards(): up_part = lax.all_gather(swapped[:, 3 * part:], 'dp', axis=0, tiled=True)  46.4 us
    all_gather x1, blocking collectives, shards(): lax.all_gather(smalls, both, axis=0, tiled=True).astype(jnp.float32)  40.8 us
    unnamed x1, blocking collectives  40.7 us
    all_gather x1, waiting for transfers between devices, shards(): out_full = lax.all_gather(out_weight, both, axis=0, tiled=True)  40.1 us
    reduce_scatter x1, waiting for transfers between devices, shards(): lax.psum_scatter(jnp.dot(act_rows, down_part, preferred_element_type=jnp....  26.1 us
    reduce_scatter x1, waiting for transfers between devices, shards(): lax.psum_scatter(back_product(grad_proj, qkv_part).astype(jnp.bfloat16),...  23.7 us
  transfers between devices with their start and end apart: 17, of which 15 were waited for; matrix products, arithmetic and copies ran while one was open for 10% of the time, Pallas kernels for 0%

commit v1 on v0

--- a/solution.py
+++ b/solution.py
@@ -6,6 +6,28 @@
 HEAD_DIM = 64
 EPSILON = 1e-05
 GELU_COEF = 0.7978845608028654
+
+
+def joined_along(blocks, dim):
+    blocks = jnp.moveaxis(blocks, 0, dim)
+    shape = blocks.shape
+    return blocks.reshape(*shape[:dim], shape[dim] * shape[dim + 1], *shape[dim + 2 :])
+
+
+def collect(array, axis, dim):
+    size = lax.axis_size(axis)
+    pairs = [(i, (i + 1) % size) for i in range(size)]
+    back = [(b, a) for a, b in pairs]
+    lower, upper = ([], [])
+    for step in range(size - 1):
+        if step % 2 == 0:
+            lower.append(lax.ppermute(lower[-1] if lower else array, axis, pairs))
+        else:
+            upper.append(lax.ppermute(upper[-1] if upper else array, axis, back))
+    blocks = jnp.stack([*lower[::-1], array, *upper])
+    shift = lax.axis_index(axis) - len(lower)
+    blocks = blocks[(jnp.arange(size) - shift) % size]
+    return joined_along(blocks, dim)
 
 
 def gelu_parts(inputs):
@@ -104,7 +126,7 @@
     streams = lax.all_gather(jnp.stack([tokens, cotangent]), "ctx", axis=1, tiled=True)
     qkv_part = lax.all_gather(swapped[:, : 3 * part], "dp", axis=0, tiled=True)
     out_full = lax.all_gather(out_weight, both, axis=0, tiled=True)
-    up_part = lax.all_gather(swapped[:, 3 * part :], "dp", axis=0, tiled=True)
+    up_part = collect(swapped[:, 3 * part :], "dp", 0)
     down_part = lax.all_gather(down_weight, "dp", axis=0, tiled=True)
     tokens_span, cot_span = (streams[0], streams[1])
     block_ranks = tract_order[0]

time: 667 us -> 629 us (0.943)
  waiting for transfers between devices: 459 us -> 395 us
  starting transfers between devices: 9.33 us -> 29.1 us
    all_gather x1 -> x0, waiting for transfers between devices: 46.4 us -> none  [shards(): up_part = lax.all_gather(swapped[:, 3 * part:], 'dp', axis=0, tiled=True)]
    all_gather x1, waiting for transfers between devices: 46.5 us -> 14.3 us  [shards(): down_part = lax.all_gather(down_weight, 'dp', axis=0, tiled=True)]
    ppermute x0 -> x7, waiting for transfers between devices: none -> 31.2 us  [the longest x4 31.2 us: collect(): lower.append(lax.ppermute(lower[-1] if lower else array, axis, pairs))]
    ppermute x0 -> x7, starting transfers between devices: none -> 20 us  [the longest x3 13.5 us: collect(): upper.append(lax.ppermute(upper[-1] if upper else array, axis, back))]
    all_gather x1, waiting for transfers between devices: 17.2 us -> 0.01 us  [shards(): lax.all_gather((normed_two * gains[1] + shifts[1]).astype(jnp.bfloat16),...]
  transfers between devices with their start and end apart: 17 -> 23, of which waited for: 15 -> 17; matrix products, arithmetic and copies ran while one was open for 10% -> 11% of each run, Pallas kernels for 0% -> 0%
where the time goes in v1:
time: 629 us; the launch traced here: 628 us
  waiting for transfers between devices  395 us (63%)
  blocking collectives  94.8 us (15%)
  matrix products  48.1 us (8%)
  starting transfers between devices  29.1 us (5%)
  local copies, waits for them, and re-layouts  26.4 us (4%)
  other arithmetic  20 us (3%)
  between operations  14.7 us (2%)
    reduce_scatter x4, waiting for transfers between devices, over_dp(): lax.psum_scatter(outer_sum(former, latter).astype(jnp.bfloat16), 'dp', sc...  203 us
    all_gather x1, blocking collectives, shards(): lax.all_gather(smalls, both, axis=0, tiled=True).astype(jnp.float32)  40.8 us
    unnamed x1, blocking collectives  40.7 us
    all_gather x1, waiting for transfers between devices, shards(): out_full = lax.all_gather(out_weight, both, axis=0, tiled=True)  40.1 us
    ppermute x4, waiting for transfers between devices, collect(): lower.append(lax.ppermute(lower[-1] if lower else array, axis, pairs))  31.2 us
    reduce_scatter x1, waiting for transfers between devices, shards(): lax.psum_scatter(jnp.dot(act_rows, down_part, preferred_element_type=jnp....  26.1 us
    reduce_scatter x1, waiting for transfers between devices, shards(): lax.psum_scatter(back_product(grad_proj, qkv_part).astype(jnp.bfloat16),...  24 us
    reduce_scatter x1, waiting for transfers between devices, shards(): lax.psum_scatter(back_product(grad_pre_low, up_part).astype(jnp.bfloat16)...  18.6 us
  transfers between devices with their start and end apart: 23, of which 17 were waited for; matrix products, arithmetic and copies ran while one was open for 11% of the time, Pallas kernels for 0%

profile of v1, /device:TPU:0, one launch (start us, length us, event | category | flops | bytes accessed | tf_op | source)
XLA Modules:
  0.0 628.2 jit_solution(12731028794834879494)
XLA Ops:
  11.1 13.2 %all_to_all.29 = bf16[4,32,1792]{2,1,0:T(8,128)(2,1)S(1)} all-to-all(bf16[4,32,1792]{2,1,0:T(8,128)(2,1)S(1)} %pad_maximum_fusion.2), channel_id=1, replica_groups=mesh['dp'=8,'ctx'=4] {'ctx'}, dimensions={0} | all-to-all | bytes 917504 | tf_op jit(solution)/shard_map/all_to_all | solution.py:123
  26.1 40.8 %all-gather.1 = bf16[32,1,384]{2,1,0:T(2,128)(2,1)S(1)} all-gather(bf16[1,1,384]{2,1,0:T(2,128)(2,1)S(1)} %reshape.466), channel_id=2, replica_groups=mesh['dp'=8,'ctx'=4] {'dp','ctx'}, dimensions={0}, use_global_device_ids=true | all-gather | bytes 25344 | tf_op jit(solution)/shard_map/all_gather | solution.py:101
  73.9 9.6 %all-gather.11.cloned.1.call-done = bf16[1024,768]{1,0:T(8,128)(2,1)} async-done(((bf16[128,768]{1,0:T(8,128)(2,1)}), bf16[1024,768]{1,0:T(8,128)(2,1)}) %all-gather.11.cloned.1.call-update) | async-done | bytes 1572880 | tf_op jit(solution)/shard_map/all_gather | solution.py:127
  91.6 3.4 all-to-all-start.1
  95.3 5.7 all-to-all-done.1
  101.0 40.1 %all-gather.13.cloned.1.call-done = bf16[1024,1024]{1,0:T(8,128)(2,1)} async-done(((bf16[32,1024]{1,0:T(8,128)(2,1)}), bf16[1024,1024]{1,0:T(8,128)(2,1)}) %all-gather.13.cloned.1.call-update) | async-done | bytes 2097168 | tf_op jit(solution)/shard_map/all_gather | solution.py:128
  146.5 9.7 %collective-permute-done = bf16[128,1024]{1,0:T(8,128)(2,1)S(1)} collective-permute-done((bf16[128,1024]{1,0:T(8,128)(2,1)S(1)}, bf16[128,1024]{1,0:T(8,128)(2,1)S(1)}, u32[]{:S(2)}, u32[]{:S(2)}) %collective-permute-start) | collective-permute-done | bytes 262176 | tf_op jit(solution)/shard_map/ppermute | solution.py:24
  156.2 4.7 collective-permute-start.4
  160.9 6.3 collective-permute-done.1
  169.7 5.8 collective-permute-start.5
  175.4 7.9 %collective-permute-done.2 = bf16[128,1024]{1,0:T(8,128)(2,1)S(1)} collective-permute-done((bf16[128,1024]{1,0:T(8,128)(2,1)S(1)}, bf16[128,1024]{1,0:T(8,128)(2,1)S(1)}, u32[]{:S(2)}, u32[]{:S(2)}) %collective-permute-start.2) | collective-permute-done | bytes 262176 | tf_op jit(solution)/shard_map/ppermute | solution.py:24
  185.9 3.0 collective-permute-start.6
  188.9 7.4 %collective-permute-done.3 = bf16[128,1024]{1,0:T(8,128)(2,1)} collective-permute-done((bf16[128,1024]{1,0:T(8,128)(2,1)S(1)}, bf16[128,1024]{1,0:T(8,128)(2,1)}, u32[]{:S(2)}, u32[]{:S(2)}) %collective-permute-start.3) | collective-permute-done | bytes 262176 | tf_op jit(solution)/shard_map/ppermute | solution.py:24
  203.4 4.7 fusion.84
  208.1 14.3 %all-gather.17.cloned.1.call-done = bf16[1024,1024]{1,0:T(8,128)(2,1)} async-done(((bf16[128,1024]{1,0:T(8,128)(2,1)}), bf16[1024,1024]{1,0:T(8,128)(2,1)}) %all-gather.17.cloned.1.call-update) | async-done | bytes 2097168 | tf_op jit(solution)/shard_map/all_gather | solution.py:130
  222.4 4.7 fusion.83
  230.5 4.7 convolution_convert_fusion.5
  235.4 18.6 %reduce-scatter.10.cloned.1.call-done = bf16[128,1024]{1,0:T(8,128)(2,1)} async-done(((bf16[512,1024]{1,0:T(8,128)(2,1)}), bf16[128,1024]{1,0:T(8,128)(2,1)}) %reduce-scatter.10.cloned.1.call-update) | async-done | bytes 262160 | tf_op jit(solution)/shard_map/reduce_scatter | solution.py:181
  255.2 26.1 %reduce-scatter.8.cloned.1.call-done = bf16[128,1024]{1,0:T(8,128)(2,1)} async-done(((bf16[512,1024]{1,0:T(8,128)(2,1)}), bf16[128,1024]{1,0:T(8,128)(2,1)}) %reduce-scatter.8.cloned.1.call-update) | async-done | bytes 262160 | tf_op jit(solution)/shard_map/reduce_scatter | solution.py:189
  284.3 16.8 %all-gather.19.cloned.1.call-done = bf16[512,1024]{1,0:T(8,128)(2,1)} async-done(((bf16[128,1024]{1,0:T(8,128)(2,1)}), bf16[512,1024]{1,0:T(8,128)(2,1)}) %all-gather.19.cloned.1.call-update) | async-done | bytes 1048592 | tf_op jit(solution)/shard_map/all_gather | solution.py:198
  303.7 4.6 convolution_convert_fusion
  311.1 3.8 multiply_convert_fusion
  321.2 4.2 convolution_convert_fusion.1
  325.5 3.4 convolution_convert_fusion.2
  331.1 36.6 %reduce-scatter.18.cloned.1.call-done = bf16[32,1024]{1,0:T(8,128)(2,1)} async-done(((bf16[256,1024]{1,0:T(8,128)(2,1)}), bf16[32,1024]{1,0:T(8,128)(2,1)}) %reduce-scatter.18.cloned.1.call-update) | async-done | bytes 65552 | tf_op jit(solution)/shard_map/reduce_scatter | solution.py:236
  369.9 68.5 %reduce-scatter.20.cloned.1.call-done = bf16[128,1024]{1,0:T(8,128)(2,1)} async-done(((bf16[1024,1024]{1,0:T(8,128)(2,1)}), bf16[128,1024]{1,0:T(8,128)(2,1)}) %reduce-scatter.20.cloned.1.call-update) | async-done | bytes 262160 | tf_op jit(solution)/shard_map/reduce_scatter | solution.py:236
  440.9 24.0 %reduce-scatter.12.cloned.1.call-done = bf16[128,1024]{1,0:T(8,128)(2,1)} async-done(((bf16[512,1024]{1,0:T(8,128)(2,1)}), bf16[128,1024]{1,0:T(8,128)(2,1)}) %reduce-scatter.12.cloned.1.call-update) | async-done | bytes 262160 | tf_op jit(solution)/shard_map/reduce_scatter | solution.py:226
  466.7 40.7 %all-reduce = f32[32,384]{1,0:T(8,128)S(1)} all-reduce(f32[32,384]{1,0:T(8,128)S(1)} %pad_maximum_fusion.6), channel_id=10, replica_groups=mesh['dp'=8,'ctx'=4] {'dp','ctx'}, use_global_device_ids=true, to_apply=%region_28.29.clone | all-reduce | flops 12288 | bytes 98304
  507.4 29.9 %reduce-scatter.16.cloned.1.call-done = bf16[128,1024]{1,0:T(8,128)(2,1)} async-done(((bf16[1024,1024]{1,0:T(8,128)(2,1)}), bf16[128,1024]{1,0:T(8,128)(2,1)}) %reduce-scatter.16.cloned.1.call-update) | async-done | bytes 262160 | tf_op jit(solution)/shard_map/reduce_scatter | solution.py:236
  537.3 68.0 %reduce-scatter.14.cloned.1.call-done = bf16[128,768]{1,0:T(8,128)(2,1)} async-done(((bf16[1024,768]{1,0:T(8,128)(2,1)}), bf16[128,768]{1,0:T(8,128)(2,1)}) %reduce-scatter.14.cloned.1.call-update) | async-done | bytes 196624 | tf_op jit(solution)/shard_map/reduce_scatter | solution.py:236
  607.1 3.5 all-to-all-start.2
  614.3 4.4 all-to-all-done.2
  (239 shorter events, 74.5 us)
Async XLA Ops:
  7.2 63.4 %all-gather.9.cloned.1.call-start = ((), (), s32[]{:S(2)}) async-start(), calls=%async_computation.10 | async-start | bytes 2621440 | tf_op jit(solution)/shard_map/all_gather | solution.py:126
  9.2 74.3 %all-gather.11.cloned.1.call-start = ((), (), s32[]{:S(2)}) async-start(), calls=%async_computation.11 | async-start | bytes 1769472 | tf_op jit(solution)/shard_map/all_gather | solution.py:127
  10.7 58.0 %copy-start.22 = (s32[1,512]{1,0:T(1,128)S(1)}, s32[1,512]{1,0:T(1,128)}, u32[]{:S(2)}) copy-start(s32[1,512]{1,0:T(1,128)} %param.14) | copy-start | bytes 6148
  10.7 58.7 %copy-start.28 = (s32[1,8]{1,0:T(1,128)S(1)}, s32[1,8]{1,0:T(1,128)}, u32[]{:S(2)}) copy-start(s32[1,8]{1,0:T(1,128)} %param.15) | copy-start | bytes 100
  25.0 116.1 %all-gather.13.cloned.1.call-start = ((), (), s32[]{:S(2)}) async-start(), calls=%async_computation.12 | async-start | bytes 2162688 | tf_op jit(solution)/shard_map/all_gather | solution.py:128
  89.9 51.2 %copy-start = (bf16[128,1024]{1,0:T(8,128)(2,1)S(1)}, bf16[128,1024]{1,0:T(8,128)(2,1)}, u32[]{:S(2)}) copy-start(bf16[128,1024]{1,0:T(8,128)(2,1)} %param.12) | copy-start | bytes 786436
  90.8 52.4 %copy-start.8 = (bf16[512,4,64]{0,2,1:T(8,128)(2,1)}, bf16[512,4,64]{0,2,1:T(8,128)(2,1)S(1)}, u32[]{:S(2)}) copy-start(bf16[512,4,64]{0,2,1:T(8,128)(2,1)S(1)} %fusion.37) | copy-start | bytes 786436
  91.6 9.4 %all-to-all-start.1 = ((bf16[4,128,256]{1,2,0:T(8,128)(2,1)}), bf16[4,128,256]{1,2,0:T(8,128)(2,1)S(1)}, u32[]{:S(2)}, u32[]{:S(2)}) async-start(bf16[4,128,256]{1,2,0:T(8,128)(2,1)} %copy.66), calls=%async_computation.1 | async-start | bytes 524288 | tf_op jit(solution)/shard_map/all_to_all | solution.py:165
  95.0 108.4 %all-gather.15.cloned.1.call-start = ((), (), s32[]{:S(2)}) async-start(), calls=%async_computation.13 | async-start | bytes 1310720 | tf_op jit(solution)/shard_map/all_gather | solution.py:171
  144.3 78.0 %all-gather.17.cloned.1.call-start = ((), (), s32[]{:S(2)}) async-start(), calls=%async_computation.14 | async-start | bytes 2359296 | tf_op jit(solution)/shard_map/all_gather | solution.py:130
  144.9 109.0 %reduce-scatter.10.cloned.1.call-start = ((), (), s32[]{:S(2)}) async-start(), calls=%async_computation.16 | async-start | bytes 1310720 | tf_op jit(solution)/shard_map/reduce_scatter | solution.py:181
  145.0 11.2 %collective-permute-start = (bf16[128,1024]{1,0:T(8,128)(2,1)S(1)}, bf16[128,1024]{1,0:T(8,128)(2,1)S(1)}, u32[]{:S(2)}, u32[]{:S(2)}) collective-permute-start(bf16[128,1024]{1,0:T(8,128)(2,1)S(1)} %slice.151), channel_id=1, source_target_pairs={{0,4},{4,8},{8,12},{12,16},{16,20},{20,24},{24,28},{28,0},{1,5},{5... | collective-permute-start | bytes 786440 | tf_op jit(solution)/shard_map/ppermute | solution.py:24
  156.2 32.7 %copy-start.16 = (bf16[128,1024]{1,0:T(8,128)(2,1)}, bf16[128,1024]{1,0:T(8,128)(2,1)S(1)}, u32[]{:S(2)}) copy-start(bf16[128,1024]{1,0:T(8,128)(2,1)S(1)} %collective-permute-done) | copy-start | bytes 786436
  156.2 11.0 %collective-permute-start.1 = (bf16[128,1024]{1,0:T(8,128)(2,1)S(1)}, bf16[128,1024]{1,0:T(8,128)(2,1)S(1)}, u32[]{:S(2)}, u32[]{:S(2)}) collective-permute-start(bf16[128,1024]{1,0:T(8,128)(2,1)S(1)} %collective-permute-done), channel_id=1, source_target_pairs={{0,4},{4,8},{8,12},{12,16},{16,20},{20,24},{24,28},{28,0},{1,5},{5... | collective-permute-start | bytes 786440 | tf_op jit(solution)/shard_map/ppermute | solution.py:24
  156.2 13.5 %collective-permute-start.4 = (bf16[128,1024]{1,0:T(8,128)(2,1)S(1)}, bf16[128,1024]{1,0:T(8,128)(2,1)S(1)}, u32[]{:S(2)}, u32[]{:S(2)}) collective-permute-start(bf16[128,1024]{1,0:T(8,128)(2,1)S(1)} %slice.151), channel_id=1, source_target_pairs={{4,0},{8,4},{12,8},{16,12},{20,16},{24,20},{28,24},{0,28},{5,1},{9... | collective-permute-start | bytes 786440 | tf_op jit(solution)/shard_map/ppermute | solution.py:26
  167.2 21.7 %copy-start.19 = (bf16[128,1024]{1,0:T(8,128)(2,1)}, bf16[128,1024]{1,0:T(8,128)(2,1)S(1)}, u32[]{:S(2)}) copy-start(bf16[128,1024]{1,0:T(8,128)(2,1)S(1)} %collective-permute-done.1) | copy-start | bytes 786436
  167.2 16.1 %collective-permute-start.2 = (bf16[128,1024]{1,0:T(8,128)(2,1)S(1)}, bf16[128,1024]{1,0:T(8,128)(2,1)S(1)}, u32[]{:S(2)}, u32[]{:S(2)}) collective-permute-start(bf16[128,1024]{1,0:T(8,128)(2,1)S(1)} %collective-permute-done.1), channel_id=1, source_target_pairs={{0,4},{4,8},{8,12},{12,16},{16,20},{20,24},{24,28},{28,0},{1,5},{5... | collective-permute-start | bytes 786440 | tf_op jit(solution)/shard_map/ppermute | solution.py:24
  169.7 19.2 %copy-start.17 = (bf16[128,1024]{1,0:T(8,128)(2,1)}, bf16[128,1024]{1,0:T(8,128)(2,1)S(1)}, u32[]{:S(2)}) copy-start(bf16[128,1024]{1,0:T(8,128)(2,1)S(1)} %collective-permute-done.4) | copy-start | bytes 786436
  169.7 16.2 %collective-permute-start.5 = (bf16[128,1024]{1,0:T(8,128)(2,1)S(1)}, bf16[128,1024]{1,0:T(8,128)(2,1)}, u32[]{:S(2)}, u32[]{:S(2)}) collective-permute-start(bf16[128,1024]{1,0:T(8,128)(2,1)S(1)} %collective-permute-done.4), channel_id=1, source_target_pairs={{4,0},{8,4},{12,8},{16,12},{20,16},{24,20},{28,24},{0,28},{5,1},{9... | collective-permute-start | bytes 786440 | tf_op jit(solution)/shard_map/ppermute | solution.py:26
  183.3 13.0 %collective-permute-start.3 = (bf16[128,1024]{1,0:T(8,128)(2,1)S(1)}, bf16[128,1024]{1,0:T(8,128)(2,1)}, u32[]{:S(2)}, u32[]{:S(2)}) collective-permute-start(bf16[128,1024]{1,0:T(8,128)(2,1)S(1)} %collective-permute-done.2), channel_id=1, source_target_pairs={{0,4},{4,8},{8,12},{12,16},{16,20},{20,24},{24,28},{28,0},{1,5},{5... | collective-permute-start | bytes 786440 | tf_op jit(solution)/shard_map/ppermute | solution.py:24
  185.9 15.5 %collective-permute-start.6 = (bf16[128,1024]{1,0:T(8,128)(2,1)}, bf16[128,1024]{1,0:T(8,128)(2,1)S(1)}, u32[]{:S(2)}, u32[]{:S(2)}) collective-permute-start(bf16[128,1024]{1,0:T(8,128)(2,1)} %collective-permute-done.5), channel_id=1, source_target_pairs={{4,0},{8,4},{12,8},{16,12},{20,16},{24,20},{28,24},{0,28},{5,1},{9... | collective-permute-start | bytes 786440 | tf_op jit(solution)/shard_map/ppermute | solution.py:26
  203.4 19.0 %copy-start.2 = (bf16[2,512,1024]{2,1,0:T(8,128)(2,1)S(1)}, bf16[2,512,1024]{2,1,0:T(8,128)(2,1)}, u32[]{:S(2)}) copy-start(bf16[2,512,1024]{2,1,0:T(8,128)(2,1)} %all-gather.9.cloned.1.call-done) | copy-start | bytes 6291460
  230.5 50.8 %reduce-scatter.8.cloned.1.call-start = ((), (), s32[]{:S(2)}) async-start(), calls=%async_computation.15 | async-start | bytes 1310720 | tf_op jit(solution)/shard_map/reduce_scatter | solution.py:189
  235.2 65.8 %all-gather.19.cloned.1.call-start = ((), (), s32[]{:S(2)}) async-start(), calls=%async_computation.17 | async-start | bytes 1310720 | tf_op jit(solution)/shard_map/all_gather | solution.py:198
  284.2 83.5 %reduce-scatter.18.cloned.1.call-start = ((), (), s32[]{:S(2)}) async-start(), calls=%async_computation.21 | async-start | bytes 589824 | tf_op jit(solution)/shard_map/reduce_scatter | solution.py:236
  303.7 134.8 %reduce-scatter.20.cloned.1.call-start = ((), (), s32[]{:S(2)}) async-start(), calls=%async_computation.22 | async-start | bytes 2359296 | tf_op jit(solution)/shard_map/reduce_scatter | solution.py:236
  308.3 156.6 %reduce-scatter.12.cloned.1.call-start = ((), (), s32[]{:S(2)}) async-start(), calls=%async_computation.18 | async-start | bytes 1310720 | tf_op jit(solution)/shard_map/reduce_scatter | solution.py:226
  321.1 216.2 %reduce-scatter.16.cloned.1.call-start = ((), (), s32[]{:S(2)}) async-start(), calls=%async_computation.20 | async-start | bytes 2359296 | tf_op jit(solution)/shard_map/reduce_scatter | solution.py:236
  325.4 279.9 %reduce-scatter.14.cloned.1.call-start = ((), (), s32[]{:S(2)}) async-start(), calls=%async_computation.19 | async-start | bytes 1769472 | tf_op jit(solution)/shard_map/reduce_scatter | solution.py:236
  367.7 72.5 %collective-permute-start.7 = (bf16[32,1024]{1,0:T(8,128)(2,1)}, bf16[32,1024]{1,0:T(8,128)(2,1)S(1)}, u32[]{:S(2)}, u32[]{:S(2)}) collective-permute-start(bf16[32,1024]{1,0:T(8,128)(2,1)} %reduce-scatter.18.cloned.1.call-done), channel_id=1, source_target_pairs={{0,0},{1,8},{2,16},{3,24},{4,1},{5,9},{6,17},{7,25},{8,2},{9,10},{... | collective-permute-start | bytes 196616 | tf_op jit(solution)/shard_map/ppermute | solution.py:244
  464.9 148.3 %copy-start.10 = (bf16[128,1024]{1,0:T(8,128)(2,1)S(1)}, bf16[128,1024]{1,0:T(8,128)(2,1)}, u32[]{:S(2)}) copy-start(bf16[128,1024]{1,0:T(8,128)(2,1)} %reduce-scatter.12.cloned.1.call-done) | copy-start | bytes 786436
  607.1 11.6 %all-to-all-start.2 = ((bf16[4,32,1792]{2,1,0:T(8,128)(2,1)}), bf16[4,32,1792]{2,1,0:T(8,128)(2,1)S(1)}, u32[]{:S(2)}, u32[]{:S(2)}) async-start(bf16[4,32,1792]{2,1,0:T(8,128)(2,1)} %bitcast.40), calls=%async_computation.7 | async-start | bytes 917504 | tf_op jit(solution)/shard_map/all_to_all | solution.py:249
  (24 other events, 136.0 us)
Sparse Core Ops, SparseCore 0:
  10.1 25.9 all-gather.8
  38.9 44.5 all-gather.10
  86.3 54.7 all-gather.12
  144.5 15.5 all-gather.14
  162.0 60.3 all-gather.16
  230.6 23.3 reduce-scatter.9
  256.5 24.7 reduce-scatter.7
  284.3 16.6 all-gather.18
  305.0 62.6 reduce-scatter.17
  371.1 67.3 reduce-scatter.19
  441.0 23.8 reduce-scatter.11
  468.3 68.9 reduce-scatter.15
  540.7 64.5 reduce-scatter.13
